TPU v7x, 32 devices: a whole 2x2x4 slice. The times are simulated.
32 devices in a mesh: grp: 1, seq: 32 (over z, y, x, core).
Axes of the slice: x: 2, y: 2, z: 4, core: 2. Of those that a mesh axis runs over, the one named last changes fastest.
Arguments:
- features: bfloat16 [8192, 768], P(('grp', 'seq')), may hold values from -6 to 6
- targets: int32 [8192, 896], P(('grp', 'seq')), may hold values from 0 to 3
- mappable: int32 [8192], P(('grp', 'seq')), may hold values 0 or 1
- w_in: bfloat16 [2, 768, 384], replicated, may hold values from -0.21875 to 0.21875
- w_conv: bfloat16 [2, 3, 384, 384], replicated, may hold values from -0.1875 to 0.1875
- w_out: bfloat16 [2, 384, 768], replicated, may hold values from -0.3125 to 0.3125
- w_head: bfloat16 [768, 896], replicated, may hold values from -0.109375 to 0.109375
Outputs:
- grad_in: float32 [2, 768, 384], P('grp', 'seq')
- grad_conv: float32 [2, 3, 384, 384], P('grp', None, 'seq')
- grad_out: float32 [2, 384, 768], P('grp', 'seq')
All inputs are finite; a program needn't handle non-finite values. No bound on the sum of `mappable` on one device may be relied on, other than what follows from the above.
Results may differ from a plain program's by a relative error of at most 0.0075.
Values may be sent and summed in bfloat16 or wider, within the bound.
A program may use at most 128 MiB of HBM per device.

v0:
```python
import math

import jax
import jax.numpy as jnp
from jax import lax
from jax.sharding import PartitionSpec as P

FIRST_DILATION = 2048
SECOND_DILATION = 4096


TANH_COEF = 0.7978845608028654
CUBIC_COEF = 0.044715


def partner(value, axis, bit):
    mask = 2**bit
    pairs = [(source, source ^ mask) for source in range(lax.axis_size(axis))]
    return lax.ppermute(value, axis, pairs)


def shifted(value, axis, steps):
    count = lax.axis_size(axis)
    first, last = (max(0, -steps), min(count, count - steps))
    return lax.ppermute(value, axis, [(source, source + steps) for source in range(first, last)])


def gelu_value(values):
    return jax.nn.gelu(values, approximate=True)


def gelu_slope(values):
    inner = TANH_COEF * (values + CUBIC_COEF * values * values * values)
    tangent = jnp.tanh(inner)
    return 0.5 * (1.0 + tangent) + 0.5 * values * (1.0 - tangent * tangent) * TANH_COEF * (
        1.0 + 3.0 * CUBIC_COEF * values * values
    )


def strand_flip(shard_rows):
    for bit_number in range(lax.axis_size("seq").bit_length() - 1):
        shard_rows = partner(shard_rows, "seq", bit_number)
    return jnp.roll(shard_rows[::-1], shard_rows.shape[-1] // 2, axis=-1)


def apply_matrix(left, matrix, transposed):
    form = "spx,yx->spy" if transposed else "spx,xy->spy"
    return jnp.einsum(form, left, matrix, preferred_element_type=jnp.float32)


def strand_grad(left, right):
    return jnp.einsum("spx,spy->sxy", left, right, preferred_element_type=jnp.float32)


def local(features, targets, mappable, w_in, w_conv, w_out, w_head):
    rows = features.shape[0]
    devices = lax.axis_size("seq")
    dilation_list = (FIRST_DILATION, SECOND_DILATION)
    weights = []
    for layer in range(2):
        shared = (w_in[layer], w_conv[layer, 0], w_conv[layer, 1], w_conv[layer, 2], w_out[layer])
        weights.append(shared)
    stream = jnp.stack([features, strand_flip(features)])
    records = []
    for layer in range(2):
        matrix_in, tap_first, tap_middle, tap_last, matrix_out = weights[layer]
        hop_count = dilation_list[layer] // rows
        before_gelu = apply_matrix(stream, matrix_in, False)
        hidden = gelu_value(before_gelu).astype(jnp.bfloat16)
        earlier = shifted(hidden, "seq", hop_count)
        later = shifted(hidden, "seq", -hop_count)
        conv_sum = (
            apply_matrix(earlier, tap_first, False)
            + apply_matrix(hidden, tap_middle, False)
            + apply_matrix(later, tap_last, False)
        )
        middle = gelu_value(conv_sum).astype(jnp.bfloat16)
        records.append((stream, before_gelu, hidden, conv_sum, middle))
        stream = (stream.astype(jnp.float32) + apply_matrix(middle, matrix_out, False)).astype(
            jnp.bfloat16
        )
    other_strand = strand_flip(stream[1])
    joined = (0.5 * (stream[0].astype(jnp.float32) + other_strand.astype(jnp.float32))).astype(
        jnp.bfloat16
    )
    logits = jnp.dot(joined, w_head, preferred_element_type=jnp.float32)
    loss_scale = 1.0 / math.sqrt(rows * devices)
    row_weight = mappable.astype(jnp.float32)[:, None]
    logit_grad = (row_weight * (jnp.exp(logits) - targets.astype(jnp.float32)) * loss_scale).astype(
        jnp.bfloat16
    )
    incoming = (0.5 * jnp.dot(logit_grad, w_head.T, preferred_element_type=jnp.float32)).astype(
        jnp.bfloat16
    )
    cotangent = jnp.stack([incoming, strand_flip(incoming)])
    full_grads = [None, None]
    for layer in (1, 0):
        matrix_in, tap_first, tap_middle, tap_last, matrix_out = weights[layer]
        incoming_state, before_gelu, hidden, conv_sum, middle = records[layer]
        hop_count = dilation_list[layer] // rows
        strand_out = strand_grad(middle, cotangent)
        slope_mid = (apply_matrix(cotangent, matrix_out, True) * gelu_slope(conv_sum)).astype(
            jnp.bfloat16
        )
        later = shifted(slope_mid, "seq", -hop_count)
        earlier = shifted(slope_mid, "seq", hop_count)
        strand_first = strand_grad(hidden, later)
        strand_middle = strand_grad(hidden, slope_mid)
        strand_last = strand_grad(hidden, earlier)
        hidden_backward = (
            apply_matrix(later, tap_first, True)
            + apply_matrix(slope_mid, tap_middle, True)
            + apply_matrix(earlier, tap_last, True)
        )
        slope_in = (hidden_backward * gelu_slope(before_gelu)).astype(jnp.bfloat16)
        strand_in = strand_grad(incoming_state, slope_in)
        if layer == 1:
            cotangent = (
                cotangent.astype(jnp.float32) + apply_matrix(slope_in, matrix_in, True)
            ).astype(jnp.bfloat16)
        grad_in_block = strand_in[0] + strand_in[1]
        grad_out_block = strand_out[0] + strand_out[1]
        grad_conv_block = jnp.stack(
            [
                strand_first[0] + strand_first[1],
                strand_middle[0] + strand_middle[1],
                strand_last[0] + strand_last[1],
            ]
        )
        full_grads[layer] = (grad_in_block, grad_conv_block, grad_out_block)
    stacked_in = jnp.stack([full_grads[0][0], full_grads[1][0]])
    stacked_conv = jnp.stack([full_grads[0][1], full_grads[1][1]])
    stacked_out = jnp.stack([full_grads[0][2], full_grads[1][2]])
    grad_in, grad_conv, grad_out = (
        lax.psum_scatter(stacked_in, "seq", scatter_dimension=1, tiled=True),
        lax.psum_scatter(stacked_conv, "seq", scatter_dimension=2, tiled=True),
        lax.psum_scatter(stacked_out, "seq", scatter_dimension=1, tiled=True),
    )
    return (grad_in, grad_conv, grad_out)


def solution(mesh):
    in_specs = (
        P(("grp", "seq"), None),
        P(("grp", "seq"), None),
        P(("grp", "seq")),
        P(),
        P(),
        P(),
        P(),
    )
    out_specs = (P("grp", "seq", None), P("grp", None, "seq", None), P("grp", "seq", None))
    return jax.shard_map(local, mesh=mesh, in_specs=in_specs, out_specs=out_specs, check_vma=False)
```

profile of v0, /device:TPU:0, one launch (start us, length us, event | category | flops | bytes accessed | tf_op | source)
XLA Modules:
  0.0 522.7 jit_solution(12647106227070908317)
XLA Ops:
  9.4 2.8 collective-permute-start.1
  12.2 9.4 %collective-permute-done.1 = bf16[256,768]{1,0:T(8,128)(2,1)S(1)} collective-permute-done((bf16[256,768]{1,0:T(8,128)(2,1)S(1)}, bf16[256,768]{1,0:T(8,128)(2,1)S(1)}, u32[]{:S(2)}, u32[]{:S(2)}) %collective-permute-start.1) | collective-permute-done | bytes 393248 | tf_op jit(solution)/shard_map/ppermute | solution.py:19
  23.4 8.8 %collective-permute-done.2 = bf16[256,768]{1,0:T(8,128)(2,1)S(1)} collective-permute-done((bf16[256,768]{1,0:T(8,128)(2,1)S(1)}, bf16[256,768]{1,0:T(8,128)(2,1)S(1)}, u32[]{:S(2)}, u32[]{:S(2)}) %collective-permute-start.2) | collective-permute-done | bytes 393248 | tf_op jit(solution)/shard_map/ppermute | solution.py:19
  33.8 8.2 %collective-permute-done.3 = bf16[256,768]{1,0:T(8,128)(2,1)S(1)} collective-permute-done((bf16[256,768]{1,0:T(8,128)(2,1)S(1)}, bf16[256,768]{1,0:T(8,128)(2,1)S(1)}, u32[]{:S(2)}, u32[]{:S(2)}) %collective-permute-start.3) | collective-permute-done | bytes 393248 | tf_op jit(solution)/shard_map/ppermute | solution.py:19
  41.9 2.3 collective-permute-start.4
  44.2 15.9 %collective-permute-done.4 = bf16[256,768]{1,0:T(8,128)(2,1)S(1)} collective-permute-done((bf16[256,768]{1,0:T(8,128)(2,1)S(1)}, bf16[256,768]{1,0:T(8,128)(2,1)S(1)}, u32[]{:S(2)}, u32[]{:S(2)}) %collective-permute-start.4) | collective-permute-done | bytes 393248 | tf_op jit(solution)/shard_map/ppermute | solution.py:19
  63.6 4.6 collective-permute-start.5
  68.6 6.2 %collective-permute-done.6 = bf16[2,256,384]{2,1,0:T(8,128)(2,1)S(1)} collective-permute-done((bf16[2,256,384]{2,1,0:T(8,128)(2,1)S(1)}, bf16[2,256,384]{2,1,0:T(8,128)(2,1)S(1)}, u32[]{:S(2)}, u32[]{:S(2)}) %collective-permute-start.6) | collective-permute-done | bytes 393248 | tf_op jit(solution)/shard_map/ppermute | solution.py:25
  80.5 5.5 %collective-permute-start.7 = (bf16[2,256,384]{2,1,0:T(8,128)(2,1)S(1)}, bf16[2,256,384]{2,1,0:T(8,128)(2,1)S(1)}, u32[]{:S(2)}, u32[]{:S(2)}) collective-permute-start(bf16[2,256,384]{2,1,0:T(8,128)(2,1)S(1)} %get-tuple-element.19), channel_id=1, source_target_pairs={{0,16},{1,17},{2,18},{3,19},{4,20},{5,21},{6,22},{7,23},{8,24},{9,... | collective-permute-start | bytes 1179656 | tf_op jit(solution)/shard_map/ppermute | solution.py:25
  86.4 13.8 %collective-permute-done.8 = bf16[2,256,384]{2,1,0:T(8,128)(2,1)S(1)} collective-permute-done((bf16[2,256,384]{2,1,0:T(8,128)(2,1)S(1)}, bf16[2,256,384]{2,1,0:T(8,128)(2,1)S(1)}, u32[]{:S(2)}, u32[]{:S(2)}) %collective-permute-start.8) | collective-permute-done | bytes 393248 | tf_op jit(solution)/shard_map/ppermute | solution.py:25
  104.5 10.4 %collective-permute-done.10 = bf16[256,768]{1,0:T(8,128)(2,1)S(1)} collective-permute-done((bf16[256,768]{1,0:T(8,128)(2,1)S(1)}, bf16[256,768]{1,0:T(8,128)(2,1)S(1)}, u32[]{:S(2)}, u32[]{:S(2)}) %collective-permute-start.10) | collective-permute-done | bytes 393248 | tf_op jit(solution)/shard_map/ppermute | solution.py:19
  115.7 9.5 %collective-permute-done.11 = bf16[256,768]{1,0:T(8,128)(2,1)S(1)} collective-permute-done((bf16[256,768]{1,0:T(8,128)(2,1)S(1)}, bf16[256,768]{1,0:T(8,128)(2,1)S(1)}, u32[]{:S(2)}, u32[]{:S(2)}) %collective-permute-start.11) | collective-permute-done | bytes 393248 | tf_op jit(solution)/shard_map/ppermute | solution.py:19
  125.2 2.3 collective-permute-start.12
  127.5 7.7 %collective-permute-done.12 = bf16[256,768]{1,0:T(8,128)(2,1)S(1)} collective-permute-done((bf16[256,768]{1,0:T(8,128)(2,1)S(1)}, bf16[256,768]{1,0:T(8,128)(2,1)S(1)}, u32[]{:S(2)}, u32[]{:S(2)}) %collective-permute-start.12) | collective-permute-done | bytes 393248 | tf_op jit(solution)/shard_map/ppermute | solution.py:19
  135.2 3.4 collective-permute-start.13
  138.6 15.5 %collective-permute-done.13 = bf16[256,768]{1,0:T(8,128)(2,1)S(1)} collective-permute-done((bf16[256,768]{1,0:T(8,128)(2,1)S(1)}, bf16[256,768]{1,0:T(8,128)(2,1)S(1)}, u32[]{:S(2)}, u32[]{:S(2)}) %collective-permute-start.13) | collective-permute-done | bytes 393248 | tf_op jit(solution)/shard_map/ppermute | solution.py:19
  154.2 2.0 slice.153
  156.1 1.9 slice.151
  158.1 2.6 fusion.12
  163.2 10.4 %collective-permute-done.15 = bf16[256,768]{1,0:T(8,128)(2,1)S(1)} collective-permute-done((bf16[256,768]{1,0:T(8,128)(2,1)S(1)}, bf16[256,768]{1,0:T(8,128)(2,1)S(1)}, u32[]{:S(2)}, u32[]{:S(2)}) %collective-permute-start.15) | collective-permute-done | bytes 393248 | tf_op jit(solution)/shard_map/ppermute | solution.py:19
  174.4 9.5 %collective-permute-done.16 = bf16[256,768]{1,0:T(8,128)(2,1)S(1)} collective-permute-done((bf16[256,768]{1,0:T(8,128)(2,1)S(1)}, bf16[256,768]{1,0:T(8,128)(2,1)S(1)}, u32[]{:S(2)}, u32[]{:S(2)}) %collective-permute-start.16) | collective-permute-done | bytes 393248 | tf_op jit(solution)/shard_map/ppermute | solution.py:19
  184.6 8.7 %collective-permute-done.17 = bf16[256,768]{1,0:T(8,128)(2,1)S(1)} collective-permute-done((bf16[256,768]{1,0:T(8,128)(2,1)S(1)}, bf16[256,768]{1,0:T(8,128)(2,1)S(1)}, u32[]{:S(2)}, u32[]{:S(2)}) %collective-permute-start.17) | collective-permute-done | bytes 393248 | tf_op jit(solution)/shard_map/ppermute | solution.py:19
  193.4 2.4 collective-permute-start.18
  195.7 15.6 %collective-permute-done.18 = bf16[256,768]{1,0:T(8,128)(2,1)S(1)} collective-permute-done((bf16[256,768]{1,0:T(8,128)(2,1)S(1)}, bf16[256,768]{1,0:T(8,128)(2,1)S(1)}, u32[]{:S(2)}, u32[]{:S(2)}) %collective-permute-start.18) | collective-permute-done | bytes 393248 | tf_op jit(solution)/shard_map/ppermute | solution.py:19
  219.8 3.3 collective-permute-done.20
  223.5 13.0 %collective-permute-done.19 = bf16[2,256,384]{2,1,0:T(8,128)(2,1)S(1)} collective-permute-done((bf16[2,256,384]{2,1,0:T(8,128)(2,1)S(1)}, bf16[2,256,384]{2,1,0:T(8,128)(2,1)S(1)}, u32[]{:S(2)}, u32[]{:S(2)}) %collective-permute-start.19) | collective-permute-done | bytes 393248 | tf_op jit(solution)/shard_map/ppermute | solution.py:25
  244.1 3.3 copy.33
  248.9 3.5 collective-permute-done.21
  253.7 4.5 copy.30
  264.0 4.8 fusion.13
  272.3 138.8 %all-reduce.5.cloned.1.call-done = (f32[2,3,384,384]{3,0,1,2:T(2,128)}, f32[2,384,768]{2,0,1:T(2,128)}) async-done(((f32[2,3,384,384]{3,0,1,2:T(2,128)}, f32[2,384,768]{2,0,1:T(2,128)}), (f32[2,3,384,384]{3,0,1,2:T(2,128)}, f32[2,384,768]{2,0,1:T(2,128)})) %all-reduce.5.cloned.1.call-update) | async-done | bytes 5898256
  414.2 101.7 %reduce-scatter.2.cloned.1.call-done = f32[2,24,384]{2,1,0:T(8,128)} async-done(((f32[2,768,384]{2,1,0:T(8,128)}), f32[2,24,384]{2,1,0:T(8,128)}) %reduce-scatter.2.cloned.1.call-update) | async-done | bytes 73744 | tf_op jit(solution)/shard_map/reduce_scatter | solution.py:135
  (127 shorter events, 55.8 us)
Async XLA Ops:
  7.2 150.9 %copy-start = (bf16[768,896]{1,0:T(8,128)(2,1)S(1)}, bf16[768,896]{1,0:T(8,128)(2,1)}, u32[]{:S(2)}) copy-start(bf16[768,896]{1,0:T(8,128)(2,1)} %param.13) | copy-start | bytes 4128772
  7.2 53.6 %copy-start.21 = (bf16[256,768]{1,0:T(8,128)(2,1)S(1)}, bf16[256,768]{1,0:T(8,128)(2,1)}, u32[]{:S(2)}) copy-start(bf16[256,768]{1,0:T(8,128)(2,1)} %param.7) | copy-start | bytes 1179652
  7.2 53.6 %copy-start.16 = (bf16[2,768,384]{2,1,0:T(8,128)(2,1)S(1)}, bf16[2,768,384]{2,1,0:T(8,128)(2,1)}, u32[]{:S(2)}) copy-start(bf16[2,768,384]{2,1,0:T(8,128)(2,1)} %param.10) | copy-start | bytes 3538948
  7.2 403.9 %all-reduce.5.cloned.1.call-start = ((), (), s32[]{:S(2)}) async-start(), calls=%async_computation.2 | async-start | bytes 11796480
  7.2 2.1 collective-permute-start
  9.4 12.3 %collective-permute-start.1 = (bf16[256,768]{1,0:T(8,128)(2,1)S(1)}, bf16[256,768]{1,0:T(8,128)(2,1)S(1)}, u32[]{:S(2)}, u32[]{:S(2)}) collective-permute-start(bf16[256,768]{1,0:T(8,128)(2,1)S(1)} %collective-permute-done), channel_id=1, source_target_pairs={{0,2},{1,3},{2,0},{3,1},{4,6},{5,7},{6,4},{7,5},{8,10},{9,11},{10,... | collective-permute-start | bytes 1179656 | tf_op jit(solution)/shard_map/ppermute | solution.py:19
  21.6 10.6 %collective-permute-start.2 = (bf16[256,768]{1,0:T(8,128)(2,1)S(1)}, bf16[256,768]{1,0:T(8,128)(2,1)S(1)}, u32[]{:S(2)}, u32[]{:S(2)}) collective-permute-start(bf16[256,768]{1,0:T(8,128)(2,1)S(1)} %collective-permute-done.1), channel_id=1, source_target_pairs={{0,4},{1,5},{2,6},{3,7},{4,0},{5,1},{6,2},{7,3},{8,12},{9,13},{10,... | collective-permute-start | bytes 1179656 | tf_op jit(solution)/shard_map/ppermute | solution.py:19
  32.2 9.7 %collective-permute-start.3 = (bf16[256,768]{1,0:T(8,128)(2,1)S(1)}, bf16[256,768]{1,0:T(8,128)(2,1)S(1)}, u32[]{:S(2)}, u32[]{:S(2)}) collective-permute-start(bf16[256,768]{1,0:T(8,128)(2,1)S(1)} %collective-permute-done.2), channel_id=1, source_target_pairs={{0,8},{1,9},{2,10},{3,11},{4,12},{5,13},{6,14},{7,15},{8,0},{9,1},... | collective-permute-start | bytes 1179656 | tf_op jit(solution)/shard_map/ppermute | solution.py:19
  41.9 18.2 %collective-permute-start.4 = (bf16[256,768]{1,0:T(8,128)(2,1)S(1)}, bf16[256,768]{1,0:T(8,128)(2,1)S(1)}, u32[]{:S(2)}, u32[]{:S(2)}) collective-permute-start(bf16[256,768]{1,0:T(8,128)(2,1)S(1)} %collective-permute-done.3), channel_id=1, source_target_pairs={{0,16},{1,17},{2,18},{3,19},{4,20},{5,21},{6,22},{7,23},{8,24},{9,... | collective-permute-start | bytes 1179656 | tf_op jit(solution)/shard_map/ppermute | solution.py:19
  62.3 12.5 %collective-permute-start.6 = (bf16[2,256,384]{2,1,0:T(8,128)(2,1)S(1)}, bf16[2,256,384]{2,1,0:T(8,128)(2,1)S(1)}, u32[]{:S(2)}, u32[]{:S(2)}) collective-permute-start(bf16[2,256,384]{2,1,0:T(8,128)(2,1)S(1)} %get-tuple-element.17), channel_id=1, source_target_pairs={{8,0},{9,1},{10,2},{11,3},{12,4},{13,5},{14,6},{15,7},{16,8},{17,9... | collective-permute-start | bytes 1179656 | tf_op jit(solution)/shard_map/ppermute | solution.py:25
  63.6 12.4 %collective-permute-start.5 = (bf16[2,256,384]{2,1,0:T(8,128)(2,1)S(1)}, bf16[2,256,384]{2,1,0:T(8,128)(2,1)S(1)}, u32[]{:S(2)}, u32[]{:S(2)}) collective-permute-start(bf16[2,256,384]{2,1,0:T(8,128)(2,1)S(1)} %get-tuple-element.17), channel_id=1, source_target_pairs={{0,8},{1,9},{2,10},{3,11},{4,12},{5,13},{6,14},{7,15},{8,16},{9,17... | collective-permute-start | bytes 1179656 | tf_op jit(solution)/shard_map/ppermute | solution.py:25
  79.3 21.0 %collective-permute-start.8 = (bf16[2,256,384]{2,1,0:T(8,128)(2,1)S(1)}, bf16[2,256,384]{2,1,0:T(8,128)(2,1)S(1)}, u32[]{:S(2)}, u32[]{:S(2)}) collective-permute-start(bf16[2,256,384]{2,1,0:T(8,128)(2,1)S(1)} %get-tuple-element.19), channel_id=1, source_target_pairs={{16,0},{17,1},{18,2},{19,3},{20,4},{21,5},{22,6},{23,7},{24,8},{25... | collective-permute-start | bytes 1179656 | tf_op jit(solution)/shard_map/ppermute | solution.py:25
  80.5 20.1 %collective-permute-start.7 = (bf16[2,256,384]{2,1,0:T(8,128)(2,1)S(1)}, bf16[2,256,384]{2,1,0:T(8,128)(2,1)S(1)}, u32[]{:S(2)}, u32[]{:S(2)}) collective-permute-start(bf16[2,256,384]{2,1,0:T(8,128)(2,1)S(1)} %get-tuple-element.19), channel_id=1, source_target_pairs={{0,16},{1,17},{2,18},{3,19},{4,20},{5,21},{6,22},{7,23},{8,24},{9,... | collective-permute-start | bytes 1179656 | tf_op jit(solution)/shard_map/ppermute | solution.py:25
  101.0 37.5 %copy-start.15 = (s32[256]{0:T(256)S(1)}, s32[256]{0:T(256)}, u32[]{:S(2)}) copy-start(s32[256]{0:T(256)} %param.9) | copy-start | bytes 3076
  101.9 52.2 %copy-start.14 = (bf16[2,256,768]{2,1,0:T(8,128)(2,1)}, bf16[2,256,768]{2,1,0:T(8,128)(2,1)S(1)}, u32[]{:S(2)}) copy-start(bf16[2,256,768]{2,1,0:T(8,128)(2,1)S(1)} %add_convert_fusion.1) | copy-start | bytes 2359300
  102.0 1.8 collective-permute-start.9
  103.8 11.2 %collective-permute-start.10 = (bf16[256,768]{1,0:T(8,128)(2,1)S(1)}, bf16[256,768]{1,0:T(8,128)(2,1)S(1)}, u32[]{:S(2)}, u32[]{:S(2)}) collective-permute-start(bf16[256,768]{1,0:T(8,128)(2,1)S(1)} %collective-permute-done.9), channel_id=1, source_target_pairs={{0,2},{1,3},{2,0},{3,1},{4,6},{5,7},{6,4},{7,5},{8,10},{9,11},{10,... | collective-permute-start | bytes 1179656 | tf_op jit(solution)/shard_map/ppermute | solution.py:19
  114.9 10.3 %collective-permute-start.11 = (bf16[256,768]{1,0:T(8,128)(2,1)S(1)}, bf16[256,768]{1,0:T(8,128)(2,1)S(1)}, u32[]{:S(2)}, u32[]{:S(2)}) collective-permute-start(bf16[256,768]{1,0:T(8,128)(2,1)S(1)} %collective-permute-done.10), channel_id=1, source_target_pairs={{0,4},{1,5},{2,6},{3,7},{4,0},{5,1},{6,2},{7,3},{8,12},{9,13},{10,... | collective-permute-start | bytes 1179656 | tf_op jit(solution)/shard_map/ppermute | solution.py:19
  125.2 10.0 %collective-permute-start.12 = (bf16[256,768]{1,0:T(8,128)(2,1)S(1)}, bf16[256,768]{1,0:T(8,128)(2,1)S(1)}, u32[]{:S(2)}, u32[]{:S(2)}) collective-permute-start(bf16[256,768]{1,0:T(8,128)(2,1)S(1)} %collective-permute-done.11), channel_id=1, source_target_pairs={{0,8},{1,9},{2,10},{3,11},{4,12},{5,13},{6,14},{7,15},{8,0},{9,1},... | collective-permute-start | bytes 1179656 | tf_op jit(solution)/shard_map/ppermute | solution.py:19
  135.2 18.9 %collective-permute-start.13 = (bf16[256,768]{1,0:T(8,128)(2,1)S(1)}, bf16[256,768]{1,0:T(8,128)(2,1)S(1)}, u32[]{:S(2)}, u32[]{:S(2)}) collective-permute-start(bf16[256,768]{1,0:T(8,128)(2,1)S(1)} %collective-permute-done.12), channel_id=1, source_target_pairs={{0,16},{1,17},{2,18},{3,19},{4,20},{5,21},{6,22},{7,23},{8,24},{9,... | collective-permute-start | bytes 1179656 | tf_op jit(solution)/shard_map/ppermute | solution.py:19
  160.7 51.2 %copy-start.6 = (f32[2,256,384]{2,1,0:T(8,128)S(1)}, f32[2,256,384]{2,1,0:T(8,128)}, u32[]{:S(2)}) copy-start(f32[2,256,384]{2,1,0:T(8,128)} %copy-done.5) | copy-start | bytes 2359300
  160.7 1.8 collective-permute-start.14
  162.5 11.2 %collective-permute-start.15 = (bf16[256,768]{1,0:T(8,128)(2,1)S(1)}, bf16[256,768]{1,0:T(8,128)(2,1)S(1)}, u32[]{:S(2)}, u32[]{:S(2)}) collective-permute-start(bf16[256,768]{1,0:T(8,128)(2,1)S(1)} %collective-permute-done.14), channel_id=1, source_target_pairs={{0,2},{1,3},{2,0},{3,1},{4,6},{5,7},{6,4},{7,5},{8,10},{9,11},{10,... | collective-permute-start | bytes 1179656 | tf_op jit(solution)/shard_map/ppermute | solution.py:19
  173.6 10.3 %collective-permute-start.16 = (bf16[256,768]{1,0:T(8,128)(2,1)S(1)}, bf16[256,768]{1,0:T(8,128)(2,1)S(1)}, u32[]{:S(2)}, u32[]{:S(2)}) collective-permute-start(bf16[256,768]{1,0:T(8,128)(2,1)S(1)} %collective-permute-done.15), channel_id=1, source_target_pairs={{0,4},{1,5},{2,6},{3,7},{4,0},{5,1},{6,2},{7,3},{8,12},{9,13},{10,... | collective-permute-start | bytes 1179656 | tf_op jit(solution)/shard_map/ppermute | solution.py:19
  183.9 9.4 %collective-permute-start.17 = (bf16[256,768]{1,0:T(8,128)(2,1)S(1)}, bf16[256,768]{1,0:T(8,128)(2,1)S(1)}, u32[]{:S(2)}, u32[]{:S(2)}) collective-permute-start(bf16[256,768]{1,0:T(8,128)(2,1)S(1)} %collective-permute-done.16), channel_id=1, source_target_pairs={{0,8},{1,9},{2,10},{3,11},{4,12},{5,13},{6,14},{7,15},{8,0},{9,1},... | collective-permute-start | bytes 1179656 | tf_op jit(solution)/shard_map/ppermute | solution.py:19
  193.4 17.9 %collective-permute-start.18 = (bf16[256,768]{1,0:T(8,128)(2,1)S(1)}, bf16[256,768]{1,0:T(8,128)(2,1)S(1)}, u32[]{:S(2)}, u32[]{:S(2)}) collective-permute-start(bf16[256,768]{1,0:T(8,128)(2,1)S(1)} %collective-permute-done.17), channel_id=1, source_target_pairs={{0,16},{1,17},{2,18},{3,19},{4,20},{5,21},{6,22},{7,23},{8,24},{9,... | collective-permute-start | bytes 1179656 | tf_op jit(solution)/shard_map/ppermute | solution.py:19
  213.8 9.3 %collective-permute-start.20 = (bf16[2,256,384]{2,1,0:T(8,128)(2,1)S(1)}, bf16[2,256,384]{2,1,0:T(8,128)(2,1)S(1)}, u32[]{:S(2)}, u32[]{:S(2)}) collective-permute-start(bf16[2,256,384]{2,1,0:T(8,128)(2,1)S(1)} %fusion.53), channel_id=1, source_target_pairs={{0,16},{1,17},{2,18},{3,19},{4,20},{5,21},{6,22},{7,23},{8,24},{9,... | collective-permute-start | bytes 1179656 | tf_op jit(solution)/shard_map/ppermute | solution.py:25
  215.3 21.2 %collective-permute-start.19 = (bf16[2,256,384]{2,1,0:T(8,128)(2,1)S(1)}, bf16[2,256,384]{2,1,0:T(8,128)(2,1)S(1)}, u32[]{:S(2)}, u32[]{:S(2)}) collective-permute-start(bf16[2,256,384]{2,1,0:T(8,128)(2,1)S(1)} %fusion.53), channel_id=1, source_target_pairs={{16,0},{17,1},{18,2},{19,3},{20,4},{21,5},{22,6},{23,7},{24,8},{25... | collective-permute-start | bytes 1179656 | tf_op jit(solution)/shard_map/ppermute | solution.py:25
  240.1 8.3 %collective-permute-start.22 = (bf16[2,256,384]{2,1,0:T(8,128)(2,1)S(1)}, bf16[2,256,384]{2,1,0:T(8,128)(2,1)S(1)}, u32[]{:S(2)}, u32[]{:S(2)}) collective-permute-start(bf16[2,256,384]{2,1,0:T(8,128)(2,1)S(1)} %fusion.65), channel_id=1, source_target_pairs={{0,8},{1,9},{2,10},{3,11},{4,12},{5,13},{6,14},{7,15},{8,16},{9,17... | collective-permute-start | bytes 1179656 | tf_op jit(solution)/shard_map/ppermute | solution.py:25
  241.4 11.0 %collective-permute-start.21 = (bf16[2,256,384]{2,1,0:T(8,128)(2,1)S(1)}, bf16[2,256,384]{2,1,0:T(8,128)(2,1)S(1)}, u32[]{:S(2)}, u32[]{:S(2)}) collective-permute-start(bf16[2,256,384]{2,1,0:T(8,128)(2,1)S(1)} %fusion.65), channel_id=1, source_target_pairs={{8,0},{9,1},{10,2},{11,3},{12,4},{13,5},{14,6},{15,7},{16,8},{17,9... | collective-permute-start | bytes 1179656 | tf_op jit(solution)/shard_map/ppermute | solution.py:25
  258.2 257.6 %reduce-scatter.2.cloned.1.call-start = ((), (), s32[]{:S(2)}) async-start(), calls=%async_computation.1 | async-start | bytes 2433024 | tf_op jit(solution)/shard_map/reduce_scatter | solution.py:135
  270.6 245.2 %copy-start.1 = (bf16[768,896]{1,0:T(8,128)(2,1)S(1)}, bf16[768,896]{1,0:T(8,128)(2,1)}, u32[]{:S(2)}) copy-start(bf16[768,896]{1,0:T(8,128)(2,1)} %param.13) | copy-start | bytes 4128772
  (16 other events, 86.2 us)
Sparse Core Ops, SparseCore 0:
  258.3 152.6 all-reduce.4
  416.9 98.8 reduce-scatter.1
where the time goes:
time: 523 us
  waiting for transfers between devices  416 us (80%)
  starting transfers between devices  39.1 us (7%)
  matrix products  26.9 us (5%)
  local copies, waits for them, and re-layouts  21.3 us (4%)
  between operations  14.7 us (3%)
    unnamed x3, waiting for transfers between devices  139 us
    ppermute x15, waiting for transfers between devices, partner(): return lax.ppermute(value, axis, pairs)  135 us
    reduce_scatter x1, waiting for transfers between devices, local(): lax.psum_scatter(stacked_in, 'seq', scatter_dimension=1, tiled=True)  102 us
    ppermute x8, waiting for transfers between devices, shifted(): lax.ppermute(value, axis, [(source, source + steps) for source in range(f...  40.6 us
    ppermute x15, starting transfers between devices, partner(): return lax.ppermute(value, axis, pairs)  20.9 us
    ppermute x8, starting transfers between devices, shifted(): lax.ppermute(value, axis, [(source, source + steps) for source in range(f...  18.2 us
    dot_general x18, matrix products, apply_matrix(): return jnp.einsum(form, left, matrix, preferred_element_type=jnp.float32)  14.2 us
  transfers between devices with their start and end apart: 25, of which 23 were waited for; matrix products, arithmetic and copies ran while one was open for 5% of the time, Pallas kernels for 0%

commit v1 on v0

v1 whole, which is shorter than its diff:
```python
import functools
import math

import jax
import jax.numpy as jnp
from jax import lax
from jax.experimental import pallas as pl
from jax.experimental.pallas import tpu as pltpu
from jax.sharding import PartitionSpec as P

FIRST_DILATION = 2048
SECOND_DILATION = 4096

TANH_COEF = 0.7978845608028654
CUBIC_COEF = 0.044715
LANES = 128
CHUNK = 32
BF16 = jnp.bfloat16
F32 = jnp.float32


def dot(left, right):
    return jnp.dot(left, right, preferred_element_type=F32)


def dot_t(left, right):
    return lax.dot_general(left, right, (((1,), (1,)), ((), ())), preferred_element_type=F32)


def grad_dot(left, right):
    return lax.dot_general(left, right, (((0,), (0,)), ((), ())), preferred_element_type=F32)


def kernel(
    n,
    features,
    packed,
    w_in_hbm,
    w_conv_hbm,
    w_out_hbm,
    w_head_hbm,
    out_in,
    out_conv,
    out_out,
    w_in,
    w_conv,
    w_out,
    w_head,
    stream,
    tracks_in,
    hidden,
    slope_h,
    middle,
    slope_m,
    cot,
    grad_v,
    narrow,
    wide,
    joined,
    logit_grad,
    sums,
    send0,
    recv0,
    send1,
    recv1,
    send2,
    recv2,
    send3,
    recv3,
    final,
    weight_sem,
    a_send,
    a_recv,
    g_send,
    g_recv,
):
    rows, channels = features.shape
    hid = w_in.shape[2]
    tracks = w_head.shape[1]
    links = rows * n // FIRST_DILATION
    part = rows // links
    stride = n // links
    me = lax.axis_index("seq")
    high = me // stride
    low = me % stride
    core = low % 2
    bit_x = (low // 2) % 2
    bit_y = low // 4
    first = bit_x * (1 - core) + bit_y * core
    second = bit_y * (1 - core) + bit_x * core
    sibling = me + 1 - 2 * core
    peer_first = me + (1 - 2 * first) * (2 + 2 * core)
    peer_second = me + (1 - 2 * second) * (4 - 2 * core)

    def chain_peer(k):
        return lax.rem(high + k, links) * stride + low

    def remote(src, dst, send, recv, peer):
        return pltpu.make_async_remote_copy(
            src_ref=src,
            dst_ref=dst,
            send_sem=send,
            recv_sem=recv,
            device_id={"seq": peer},
            device_id_type=pl.DeviceIdType.MESH,
        )

    weight_copies = [
        pltpu.make_async_copy(src, dst, weight_sem.at[i])
        for i, (src, dst) in enumerate(
            ((w_in_hbm, w_in), (w_conv_hbm, w_conv), (w_out_hbm, w_out), (w_head_hbm, w_head))
        )
    ]
    for copy in weight_copies:
        copy.start()

    barrier = pltpu.get_barrier_semaphore()
    partners = [sibling, peer_first, peer_second] + [chain_peer(k) for k in range(1, links)]
    for peer in partners:
        pl.semaphore_signal(
            barrier, inc=1, device_id={"seq": peer}, device_id_type=pl.DeviceIdType.MESH
        )
    pl.semaphore_wait(barrier, len(partners))

    own = pl.ds(pl.multiple_of(high * part, part), part)
    regroup = [[], []]
    for which, (src, dst) in enumerate(((features, stream.at[0]), (packed, tracks_in))):
        for k in range(1, links):
            there = pl.ds(pl.multiple_of(lax.rem(high + k, links) * part, part), part)
            copy = remote(
                src.at[there], dst.at[own], a_send.at[which, k], a_recv.at[which, k], chain_peer(k)
            )
            copy.start()
            regroup[which].append(copy)
    stream[0, own, :] = features[own, :]
    tracks_in[own, :] = packed[own, :]

    def swap(value):
        half = value.shape[1] // 2
        return jnp.concatenate([value[:, half:], value[:, :half]], axis=1)

    def mirror(p):
        return rows + (links - 1 - p) * part

    def chunks(count, body):
        def step(i, carry):
            body(pl.ds(pl.multiple_of(i * CHUNK, CHUNK), CHUNK))
            return carry

        lax.fori_loop(0, count // CHUNK, step, 0)

    def chain_chunks(body):
        for p in range(links):

            def step(i, carry, p=p):
                offset = pl.multiple_of(i * CHUNK, CHUNK)
                body(pl.ds(p * part + offset, CHUNK), pl.ds(mirror(p) + offset, CHUNK))
                return carry

            lax.fori_loop(0, part // CHUNK, step, 0)

    def activate(value_ref, slope_ref, layer):
        def body(at):
            v = narrow[at, :]
            square = v * v
            tangent = jnp.tanh(TANH_COEF * (v + CUBIC_COEF * square * v))
            value_ref[layer, at, :] = (0.5 * v * (1.0 + tangent)).astype(BF16)
            slope_ref[layer, at, :] = 0.5 * (1.0 + tangent) + 0.5 * v * (
                1.0 - tangent * tangent
            ) * TANH_COEF * (1.0 + 3.0 * CUBIC_COEF * square)

        chunks(2 * rows, body)

    def strand(s):
        return slice(s * rows, (s + 1) * rows)

    def ends(s, skip):
        return slice(s * rows + skip, (s + 1) * rows), slice(s * rows, (s + 1) * rows - skip)

    steps_of = (1, SECOND_DILATION // FIRST_DILATION)

    for copy in regroup[0]:
        copy.wait()

    def spread(at, across):
        stream[0, across, :] = swap(stream[0, at, :])

    chain_chunks(spread)
    for copy in weight_copies[:3]:
        copy.wait()

    for layer in range(2):
        skip = steps_of[layer] * part
        for s in range(2):
            narrow[strand(s), :] = dot(stream[layer, strand(s), :], w_in[layer])
        activate(hidden, slope_h, layer)
        for s in range(2):
            narrow[strand(s), :] = dot(hidden[layer, strand(s), :], w_conv[layer, 1])
            after, before = ends(s, skip)
            narrow[after, :] += dot(hidden[layer, before, :], w_conv[layer, 0])
            narrow[before, :] += dot(hidden[layer, after, :], w_conv[layer, 2])
        activate(middle, slope_m, layer)
        for s in range(2):
            wide[strand(s), :] = dot(middle[layer, strand(s), :], w_out[layer])

        def add(at, layer=layer):
            stream[layer + 1, at, :] = (stream[layer, at, :].astype(F32) + wide[at, :]).astype(BF16)

        chunks(2 * rows, add)

    def join(at, across):
        joined[at, :] = (
            0.5 * (stream[2, at, :].astype(F32) + swap(stream[2, across, :]).astype(F32))
        ).astype(BF16)

    chain_chunks(join)
    weight_copies[3].wait()
    for copy in regroup[1]:
        copy.wait()
    loss_scale = 1.0 / math.sqrt(rows * n)
    for panel in range(tracks // LANES):
        at_panel = slice(panel * LANES, (panel + 1) * LANES)
        logits = dot(joined[...], w_head[:, at_panel])
        mask = tracks_in[:, tracks:].astype(F32)
        counts = tracks_in[:, at_panel].astype(F32)
        logit_grad[:, at_panel] = (mask * (jnp.exp(logits) - counts) * loss_scale).astype(BF16)
    wide[:rows, :] = dot_t(logit_grad[...], w_head[...])

    def divide(at, across):
        incoming = (0.5 * wide[at, :]).astype(BF16)
        cot[at, :] = incoming
        cot[across, :] = swap(incoming)

    chain_chunks(divide)

    quads = [(h, y, x) for h in range(links) for y in range(2) for x in range(2)]
    per_chip = 2 * hid // n

    def place(layer, half, start, value, height):
        for j, (h, y, x) in enumerate(quads):
            second_i, first_i = (y, x) if half == 0 else (x, y)
            sums[layer, half, h, second_i, first_i, start : start + height, :] = value[
                j * height : (j + 1) * height, :
            ]

    def stage0(layer):
        def step(h, carry):
            for b in range(2):
                for a in range(2):
                    send0[layer, h, b, a] = sums[layer, 1 - core, h, b, a].astype(BF16)
            return carry

        lax.fori_loop(0, links, step, 0)
        copy = remote(
            send0.at[layer], recv0.at[layer], g_send.at[layer, 0], g_recv.at[layer, 0], sibling
        )
        copy.start()
        return [copy]

    def stage1(layer, copies):
        for copy in copies:
            copy.wait()

        def step(h, carry):
            for b in range(2):
                send1[layer, h, b] = (
                    sums[layer, core, h, b, 1 - first]
                    + recv0[layer, h, b, 1 - first].astype(F32)
                ).astype(BF16)
            return carry

        lax.fori_loop(0, links, step, 0)
        copy = remote(
            send1.at[layer], recv1.at[layer], g_send.at[layer, 1], g_recv.at[layer, 1], peer_first
        )
        copy.start()
        return [copy]

    def partial1(layer, h, b):
        return (
            sums[layer, core, h, b, first]
            + recv0[layer, h, b, first].astype(F32)
            + recv1[layer, h, b].astype(F32)
        )

    def stage2(layer, copies):
        for copy in copies:
            copy.wait()

        def step(h, carry):
            send2[layer, h] = partial1(layer, h, 1 - second).astype(BF16)
            return carry

        lax.fori_loop(0, links, step, 0)
        copy = remote(
            send2.at[layer], recv2.at[layer], g_send.at[layer, 2], g_recv.at[layer, 2], peer_second
        )
        copy.start()
        return [copy]

    def partial2(layer, h):
        return partial1(layer, h, second) + recv2[layer, h].astype(F32)

    def stage3(layer, copies):
        for copy in copies:
            copy.wait()
        started = []
        for k in range(1, links):
            send3[layer, k] = partial2(layer, lax.rem(high + k, links)).astype(BF16)
            copy = remote(
                send3.at[layer, k],
                recv3.at[layer, k],
                g_send.at[layer, 3 + k],
                g_recv.at[layer, 3 + k],
                chain_peer(k),
            )
            copy.start()
            started.append(copy)
        return started

    def stage4(layer, copies):
        total = partial2(layer, high)
        for k, copy in enumerate(copies):
            copy.wait()
            total = total + recv3[layer, k + 1].astype(F32)
        final[layer, core] = total
        copy = remote(
            final.at[layer, core],
            final.at[layer, core],
            g_send.at[layer, 3],
            g_recv.at[layer, 3],
            sibling,
        )
        copy.start()
        return [copy]

    pending = None
    for layer in (1, 0):
        skip = steps_of[layer] * part
        grad = grad_dot(middle[layer], cot[...])
        place(layer, 1, per_chip, grad[:, :hid], per_chip)
        place(layer, 1, 2 * per_chip, grad[:, hid:], per_chip)
        for s in range(2):
            narrow[strand(s), :] = dot_t(cot[strand(s), :], w_out[layer])

        def slope(at, layer=layer):
            grad_v[at, :] = (narrow[at, :] * slope_m[layer, at, :]).astype(BF16)

        chunks(2 * rows, slope)
        if pending is not None:
            pending = stage1(1, pending)
        spans = [ends(s, skip) for s in range(2)]

        def joined_rows(read, side):
            return jnp.concatenate([read(spans[s][side]) for s in range(2)], axis=0)

        def read_hidden(at, layer=layer):
            return hidden[layer, at, :]

        def read_grad(at):
            return grad_v[at, :]

        place(
            layer,
            0,
            2 * per_chip,
            grad_dot(joined_rows(read_hidden, 1), joined_rows(read_grad, 0)),
            per_chip,
        )
        place(layer, 0, 3 * per_chip, grad_dot(hidden[layer], grad_v[...]), per_chip)
        place(
            layer,
            1,
            0,
            grad_dot(joined_rows(read_hidden, 0), joined_rows(read_grad, 1)),
            per_chip,
        )
        for s in range(2):
            narrow[strand(s), :] = dot_t(grad_v[strand(s), :], w_conv[layer, 1])
            after, before = ends(s, skip)
            narrow[before, :] += dot_t(grad_v[after, :], w_conv[layer, 0])
            narrow[after, :] += dot_t(grad_v[before, :], w_conv[layer, 2])

        def slope_back(at, layer=layer):
            grad_v[at, :] = (narrow[at, :] * slope_h[layer, at, :]).astype(BF16)

        chunks(2 * rows, slope_back)
        place(layer, 0, 0, grad_dot(stream[layer], grad_v[...]), 2 * per_chip)
        if layer == 1:
            pending = stage0(1)
            for s in range(2):
                wide[strand(s), :] = dot_t(grad_v[strand(s), :], w_in[layer])

            def renew(at):
                cot[at, :] = (cot[at, :].astype(F32) + wide[at, :]).astype(BF16)

            chunks(2 * rows, renew)
    other = stage0(0)
    pending = stage2(1, pending)
    other = stage1(0, other)
    pending = stage3(1, pending)
    other = stage2(0, other)
    pending = stage4(1, pending)
    other = stage3(0, other)
    other = stage4(0, other)
    for copy in pending + other:
        copy.wait()

    dev_rows = per_chip // 2
    for c in range(2):

        @pl.when(core == c)
        def _(c=c):
            for layer in range(2):
                out_in[layer] = final[layer, 0, c * per_chip : (c + 1) * per_chip, :]

                def own_rows(half, start, c=c, layer=layer):
                    block = final[layer, half, start : start + per_chip, :]
                    return block[c * dev_rows : (c + 1) * dev_rows, :]

                out_conv[layer, 0] = own_rows(0, 2 * per_chip)
                out_conv[layer, 1] = own_rows(0, 3 * per_chip)
                out_conv[layer, 2] = own_rows(1, 0)
                out_out[layer, :, :hid] = own_rows(1, per_chip)
                out_out[layer, :, hid:] = own_rows(1, 2 * per_chip)


def local(features, targets, mappable, w_in, w_conv, w_out, w_head):
    rows, channels = features.shape
    n = lax.axis_size("seq")
    links = rows * n // FIRST_DILATION
    hid = w_in.shape[2]
    tracks = targets.shape[1]
    per_chip = 2 * hid // n
    height = 4 * per_chip
    extra = jnp.broadcast_to(mappable[:, None], (rows, LANES))
    packed = jnp.concatenate([targets, extra], axis=1).astype(BF16)
    both = 2 * rows
    vmem = pl.BlockSpec(memory_space=pltpu.VMEM)
    hbm = pl.BlockSpec(memory_space=pl.ANY)
    quad = (links, 2, 2, height, hid)
    return pl.pallas_call(
        functools.partial(kernel, n),
        out_shape=(
            jax.ShapeDtypeStruct((2, channels // n, hid), F32),
            jax.ShapeDtypeStruct((2, 3, hid // n, hid), F32),
            jax.ShapeDtypeStruct((2, hid // n, channels), F32),
        ),
        in_specs=[vmem, vmem, hbm, hbm, hbm, hbm],
        out_specs=(vmem, vmem, vmem),
        scratch_shapes=[
            pltpu.VMEM(w_in.shape, BF16),
            pltpu.VMEM(w_conv.shape, BF16),
            pltpu.VMEM(w_out.shape, BF16),
            pltpu.VMEM(w_head.shape, BF16),
            pltpu.VMEM((3, both, channels), BF16),
            pltpu.VMEM((rows, tracks + LANES), BF16),
            pltpu.VMEM((2, both, hid), BF16),
            pltpu.VMEM((2, both, hid), F32),
            pltpu.VMEM((2, both, hid), BF16),
            pltpu.VMEM((2, both, hid), F32),
            pltpu.VMEM((both, channels), BF16),
            pltpu.VMEM((both, hid), BF16),
            pltpu.VMEM((both, hid), F32),
            pltpu.VMEM((both, channels), F32),
            pltpu.VMEM((rows, channels), BF16),
            pltpu.VMEM((rows, tracks), BF16),
            pltpu.VMEM((2, 2) + quad, F32),
            pltpu.VMEM((2,) + quad, BF16),
            pltpu.VMEM((2,) + quad, BF16),
            pltpu.VMEM((2, links, 2, height, hid), BF16),
            pltpu.VMEM((2, links, 2, height, hid), BF16),
            pltpu.VMEM((2, links, height, hid), BF16),
            pltpu.VMEM((2, links, height, hid), BF16),
            pltpu.VMEM((2, links, height, hid), BF16),
            pltpu.VMEM((2, links, height, hid), BF16),
            pltpu.VMEM((2, 2, height, hid), F32),
            pltpu.SemaphoreType.DMA((4,)),
            pltpu.SemaphoreType.DMA((2, links)),
            pltpu.SemaphoreType.DMA((2, links)),
            pltpu.SemaphoreType.DMA((2, 3 + links)),
            pltpu.SemaphoreType.DMA((2, 3 + links)),
        ],
        compiler_params=pltpu.CompilerParams(
            collective_id=0, has_side_effects=True, vmem_limit_bytes=60 * 1024 * 1024
        ),
    )(features, packed, w_in, w_conv, w_out, w_head)


def solution(mesh):
    in_specs = (
        P(("grp", "seq"), None),
        P(("grp", "seq"), None),
        P(("grp", "seq")),
        P(),
        P(),
        P(),
        P(),
    )
    out_specs = (P("grp", "seq", None), P("grp", None, "seq", None), P("grp", "seq", None))
    return jax.shard_map(local, mesh=mesh, in_specs=in_specs, out_specs=out_specs, check_vma=False)
```

time: 523 us -> 79 us (0.15)
  waiting for transfers between devices: 416 us -> 0 us
  Pallas kernels: 0 us -> 70.5 us
  starting transfers between devices: 39.1 us -> 0 us
  matrix products: 26.9 us -> 0 us
  local copies, waits for them, and re-layouts: 21.3 us -> 4.81 us
  between operations: 14.7 us -> 0.65 us
    ppermute x23 -> x0, waiting for transfers between devices: 175 us -> none  [the longest x15 135 us: partner(): return lax.ppermute(value, axis, pairs)]
    unnamed x3 -> x0, waiting for transfers between devices: 139 us -> none
    reduce_scatter x1 -> x0, waiting for transfers between devices: 102 us -> none  [local(): lax.psum_scatter(stacked_in, 'seq', scatter_dimension=1, tiled=True)]
    pallas_call x0 -> x1, Pallas kernels: none -> 70.5 us  [local(): pl.pallas_call(functools.partial(kernel, n), out_shape=(jax.ShapeDtypeStr...]
    ppermute x23 -> x0, starting transfers between devices: 39 us -> none  [the longest x15 20.9 us: partner(): return lax.ppermute(value, axis, pairs)]
    dot_general x29 -> x0, matrix products: 26.9 us -> none  [the longest x18 14.2 us: apply_matrix(): return jnp.einsum(form, left, matrix, preferred_element_type=jnp.float32)]
    another operation x2 -> x0, local copies, waits for them, and re-layouts: 7.79 us -> none  [the longest x1 4.5 us: local(): stacked_conv = jnp.stack([full_grads[0][1], full_grads[1][1]])]
    unnamed x49 -> x1, local copies, waits for them, and re-layouts: 8.41 us -> 1.52 us
  transfers between devices with their start and end apart: 25 -> 0, of which waited for: 23 -> 0; matrix products, arithmetic and copies ran while one was open for 5% -> 0% of each run, Pallas kernels for 0% -> 0%
where the time goes in v1:
time: 79 us; the launch traced here: 78.7 us
  Pallas kernels  70.5 us (89%)
  local copies, waits for them, and re-layouts  4.81 us (6%)
  other arithmetic  2.77 us (4%)
    pallas_call x1, Pallas kernels, local(): pl.pallas_call(functools.partial(kernel, n), out_shape=(jax.ShapeDtypeStr...  70.5 us
    pallas_call x2, local copies, waits for them, and re-layouts, local(): pl.pallas_call(functools.partial(kernel, n), out_shape=(jax.ShapeDtypeStr...  3.19 us
    another operation x2, other arithmetic  1.92 us

profile of v1, /device:TPU:0, one launch (start us, length us, event | category | flops | bytes accessed | tf_op | source)
XLA Modules:
  0.0 78.7 jit_solution(1288456847755817847)
XLA Ops:
  0.6 0.7 convert.8
  1.3 0.1 broadcast_in_dim.2
  1.4 1.2 %convert.7 = bf16[256,896]{1,0:T(8,128)(2,1)S(1)} convert(s32[256,896]{1,0:T(8,128)} %param.8) | non-fusion elementwise | flops 229376 | bytes 1376256 | tf_op jit(solution)/shard_map/convert
  2.7 0.9 %pad_maximum_fusion.packed = bf16[256,1024]{1,0:T(8,128)(2,1)} fusion(bf16[256,128]{1,0:T(8,128)(2,1)S(1)} %broadcast_in_dim.2, bf16[256,896]{1,0:T(8,128)(2,1)S(1)} %convert.7), kind=kLoop, calls=%fused_computation | loop fusion | flops 1048576 | bytes 1048576 | tf_op jit(solution)/shard_map/concatenate | solution.py:437
  3.5 70.5 %shard_map.94 = (f32[2,24,384]{2,1,0:T(8,128)}, f32[2,3,12,384]{3,2,1,0:T(8,128)}, f32[2,12,768]{2,1,0:T(8,128)}) custom-call(bf16[256,768]{1,0:T(8,128)(2,1)} %features.1, bf16[256,1024]{1,0:T(8,128)(2,1)} %pad_maximum_fusion.packed, bf16[2,768,384]{2,1,0:T(8,128)(2,1)} %w_in_hbm.1, bf16[2,3,384,384]{3,2,1,0:T(8,128)(2,1)} %w_conv_hbm.1, ...), custom_call_target="tpu_custom_call" | custom-call | tf_op jit(solution)/shard_map/pallas_call | solution.py:442
  74.0 1.6 %copy.11 = f32[2,12,768]{2,0,1:T(2,128)} copy(f32[2,12,768]{2,1,0:T(8,128)} %get-tuple-element.5) | data formatting | bytes 147456 | tf_op jit(solution)/shard_map/pallas_call | solution.py:442
  75.6 1.6 %copy.10 = f32[2,3,12,384]{3,0,2,1:T(2,128)} copy(f32[2,3,12,384]{3,2,1,0:T(8,128)} %get-tuple-element.4) | data formatting | bytes 221184 | tf_op jit(solution)/shard_map/pallas_call | solution.py:442
  77.2 1.5 %copy.13 = f32[2,24,384]{2,1,0:T(8,128)} copy(f32[2,24,384]{2,1,0:T(8,128)} %get-tuple-element.9) | data formatting | bytes 147456

commit v2 on v1

v2 whole, which is shorter than its diff:
```python
import functools
import math

import jax
import jax.numpy as jnp
from jax import lax
from jax.experimental import pallas as pl
from jax.experimental.pallas import tpu as pltpu
from jax.sharding import PartitionSpec as P

FIRST_DILATION = 2048
SECOND_DILATION = 4096

TANH_COEF = 0.7978845608028654
CUBIC_COEF = 0.044715
LANES = 128
CHUNK = 32
BF16 = jnp.bfloat16
F32 = jnp.float32


def dot(left, right):
    return jnp.dot(left, right, preferred_element_type=F32)


def dot_t(left, right):
    return lax.dot_general(left, right, (((1,), (1,)), ((), ())), preferred_element_type=F32)


def grad_dot(left, right):
    return lax.dot_general(left, right, (((0,), (0,)), ((), ())), preferred_element_type=F32)


def kernel(n, *refs):
    (features, targets, mappable, w_in_hbm, w_conv_hbm, w_out_hbm, w_head_hbm, result) = refs[:8]
    (w_in, w_conv, w_out, w_head, stream, packed, tracks_in) = refs[8:15]
    (hidden, slope_h, middle, slope_m, cot, grad_v, narrow, wide, joined, logit_grad) = refs[15:25]
    chunk_refs = (refs[25:35], refs[35:45])
    (weight_sem, a_send, a_recv, g_send, g_recv) = refs[45:]
    rows, channels = features.shape
    hid = w_in.shape[2]
    tracks = w_head.shape[1]
    links = rows * n // FIRST_DILATION
    part = rows // links
    stride = n // links
    me = lax.axis_index("seq")
    high = me // stride
    low = me % stride
    core = low % 2
    bit_x = (low // 2) % 2
    bit_y = low // 4
    first = bit_x * (1 - core) + bit_y * core
    second = bit_y * (1 - core) + bit_x * core
    sibling = me + 1 - 2 * core
    peer_first = me + (1 - 2 * first) * (2 + 2 * core)
    peer_second = me + (1 - 2 * second) * (4 - 2 * core)

    def chain_peer(k):
        return lax.rem(high + k, links) * stride + low

    def remote(src, dst, send, recv, peer):
        return pltpu.make_async_remote_copy(
            src_ref=src,
            dst_ref=dst,
            send_sem=send,
            recv_sem=recv,
            device_id={"seq": peer},
            device_id_type=pl.DeviceIdType.MESH,
        )

    weight_copies = [
        pltpu.make_async_copy(src, dst, weight_sem.at[i])
        for i, (src, dst) in enumerate(
            ((w_in_hbm, w_in), (w_conv_hbm, w_conv), (w_out_hbm, w_out), (w_head_hbm, w_head))
        )
    ]
    for copy in weight_copies:
        copy.start()

    barrier = pltpu.get_barrier_semaphore()
    partners = [sibling, peer_first, peer_second] + [chain_peer(k) for k in range(1, links)]
    for peer in partners:
        pl.semaphore_signal(
            barrier, inc=1, device_id={"seq": peer}, device_id_type=pl.DeviceIdType.MESH
        )

    def chunks(count, body):
        def step(i, carry):
            body(pl.ds(pl.multiple_of(i * CHUNK, CHUNK), CHUNK))
            return carry

        lax.fori_loop(0, count // CHUNK, step, 0)

    def pack(at):
        packed[at, :tracks] = targets[at, :].astype(F32).astype(BF16)
        packed[at, tracks:] = mappable[at, :].astype(F32).astype(BF16)

    chunks(rows, pack)
    pl.semaphore_wait(barrier, len(partners))

    own = pl.ds(pl.multiple_of(high * part, part), part)
    regroup = [[], []]
    for which, (src, dst) in enumerate(((features, stream.at[0]), (packed, tracks_in))):
        for k in range(1, links):
            there = pl.ds(pl.multiple_of(lax.rem(high + k, links) * part, part), part)
            copy = remote(
                src.at[there], dst.at[own], a_send.at[which, k], a_recv.at[which, k], chain_peer(k)
            )
            copy.start()
            regroup[which].append(copy)
    stream[0, own, :] = features[own, :]
    tracks_in[own, :] = packed[own, :]

    def swap(value):
        half = value.shape[1] // 2
        return jnp.concatenate([value[:, half:], value[:, :half]], axis=1)

    def mirror(p):
        return rows + (links - 1 - p) * part

    def chain_chunks(body):
        for p in range(links):

            def step(i, carry, p=p):
                offset = pl.multiple_of(i * CHUNK, CHUNK)
                body(pl.ds(p * part + offset, CHUNK), pl.ds(mirror(p) + offset, CHUNK))
                return carry

            lax.fori_loop(0, part // CHUNK, step, 0)

    def activate(value_ref, slope_ref, layer):
        def body(at):
            v = narrow[at, :]
            square = v * v
            tangent = jnp.tanh(TANH_COEF * (v + CUBIC_COEF * square * v))
            value_ref[layer, at, :] = (0.5 * v * (1.0 + tangent)).astype(BF16)
            slope_ref[layer, at, :] = 0.5 * (1.0 + tangent) + 0.5 * v * (
                1.0 - tangent * tangent
            ) * TANH_COEF * (1.0 + 3.0 * CUBIC_COEF * square)

        chunks(2 * rows, body)

    def strand(s):
        return slice(s * rows, (s + 1) * rows)

    def ends(s, skip):
        return slice(s * rows + skip, (s + 1) * rows), slice(s * rows, (s + 1) * rows - skip)

    steps_of = (1, SECOND_DILATION // FIRST_DILATION)

    for copy in regroup[0]:
        copy.wait()

    def spread(at, across):
        stream[0, across, :] = swap(stream[0, at, :])

    chain_chunks(spread)
    for copy in weight_copies[:3]:
        copy.wait()

    for layer in range(2):
        skip = steps_of[layer] * part
        for s in range(2):
            narrow[strand(s), :] = dot(stream[layer, strand(s), :], w_in[layer])
        activate(hidden, slope_h, layer)
        for s in range(2):
            narrow[strand(s), :] = dot(hidden[layer, strand(s), :], w_conv[layer, 1])
            after, before = ends(s, skip)
            narrow[after, :] += dot(hidden[layer, before, :], w_conv[layer, 0])
            narrow[before, :] += dot(hidden[layer, after, :], w_conv[layer, 2])
        activate(middle, slope_m, layer)
        for s in range(2):
            wide[strand(s), :] = dot(middle[layer, strand(s), :], w_out[layer])

        def add(at, layer=layer):
            stream[layer + 1, at, :] = (stream[layer, at, :].astype(F32) + wide[at, :]).astype(BF16)

        chunks(2 * rows, add)

    def join(at, across):
        joined[at, :] = (
            0.5 * (stream[2, at, :].astype(F32) + swap(stream[2, across, :]).astype(F32))
        ).astype(BF16)

    chain_chunks(join)
    weight_copies[3].wait()
    for copy in regroup[1]:
        copy.wait()
    loss_scale = 1.0 / math.sqrt(rows * n)
    for panel in range(tracks // LANES):
        at_panel = slice(panel * LANES, (panel + 1) * LANES)
        logits = dot(joined[...], w_head[:, at_panel])
        mask = tracks_in[:, tracks:].astype(F32)
        counts = tracks_in[:, at_panel].astype(F32)
        logit_grad[:, at_panel] = (mask * (jnp.exp(logits) - counts) * loss_scale).astype(BF16)
    wide[:rows, :] = dot_t(logit_grad[...], w_head[...])

    def divide(at, across):
        incoming = (0.5 * wide[at, :]).astype(BF16)
        cot[at, :] = incoming
        cot[across, :] = swap(incoming)

    chain_chunks(divide)

    quads = [(h, y, x) for h in range(links) for y in range(2) for x in range(2)]
    per_chip = 2 * hid // n

    def place(layer, chunk, start, value, height):
        sums = chunk_refs[chunk][0]
        limit = sums.shape[5]
        for half in range(2):
            low_row = max(start, half * limit)
            high_row = min(start + height, (half + 1) * limit)
            if low_row >= high_row:
                continue
            at = slice(low_row - half * limit, high_row - half * limit)
            for j, (h, y, x) in enumerate(quads):
                b, a = (y, x) if half == 0 else (x, y)
                base = j * height - start
                sums[layer, half, h, b, a, at, :] = value[base + low_row : base + high_row, :]

    class Scatter:
        def __init__(self, layer, chunk):
            (self.sums, *pairs, self.final) = chunk_refs[chunk]
            self.send, self.recv = pairs[0::2], pairs[1::2]
            self.layer, self.index = layer, 2 * layer + chunk
            self.stage, self.copies = 0, []

        def start(self, src, dst, sem, peer):
            copy = remote(src, dst, g_send.at[self.index, sem], g_recv.at[self.index, sem], peer)
            copy.start()
            self.copies.append(copy)

        def finish(self):
            for copy in self.copies:
                copy.wait()
            self.copies = []

        def advance(self):
            self.finish()
            getattr(self, "stage%d" % self.stage)()
            self.stage += 1

        def stage0(self):
            def step(h, carry):
                for b in range(2):
                    for a in range(2):
                        self.send[0][self.layer, h, b, a] = self.sums[
                            self.layer, 1 - core, h, b, a
                        ].astype(BF16)
                return carry

            lax.fori_loop(0, links, step, 0)
            self.start(self.send[0].at[self.layer], self.recv[0].at[self.layer], 0, sibling)

        def partial0(self, h, b, a):
            return self.sums[self.layer, core, h, b, a] + self.recv[0][
                self.layer, h, b, a
            ].astype(F32)

        def partial1(self, h, b):
            return self.partial0(h, b, first) + self.recv[1][self.layer, h, b].astype(F32)

        def partial2(self, h):
            return self.partial1(h, second) + self.recv[2][self.layer, h].astype(F32)

        def stage1(self):
            def step(h, carry):
                for b in range(2):
                    self.send[1][self.layer, h, b] = self.partial0(h, b, 1 - first).astype(BF16)
                return carry

            lax.fori_loop(0, links, step, 0)
            self.start(self.send[1].at[self.layer], self.recv[1].at[self.layer], 1, peer_first)

        def stage2(self):
            def step(h, carry):
                self.send[2][self.layer, h] = self.partial1(h, 1 - second).astype(BF16)
                return carry

            lax.fori_loop(0, links, step, 0)
            self.start(self.send[2].at[self.layer], self.recv[2].at[self.layer], 2, peer_second)

        def stage3(self):
            for k in range(1, links):
                self.send[3][self.layer, k] = self.partial2(lax.rem(high + k, links)).astype(BF16)
                self.start(
                    self.send[3].at[self.layer, k],
                    self.recv[3].at[self.layer, k],
                    3 + k,
                    chain_peer(k),
                )

        def stage4(self):
            total = self.partial2(high)
            for k in range(1, links):
                total = total + self.recv[3][self.layer, k].astype(F32)
            self.final[self.layer, core] = total
            here = self.final.at[self.layer, core]
            self.start(here, here, 3, sibling)

    wide_1, tall_1, wide_0, tall_0 = [Scatter(layer, chunk) for layer in (1, 0) for chunk in (0, 1)]

    for layer in (1, 0):
        skip = steps_of[layer] * part
        grad = grad_dot(middle[layer], cot[...])
        place(layer, 0, 3 * per_chip, grad[:, :hid], per_chip)
        place(layer, 0, 4 * per_chip, grad[:, hid:], per_chip)
        for s in range(2):
            narrow[strand(s), :] = dot_t(cot[strand(s), :], w_out[layer])

        def slope(at, layer=layer):
            grad_v[at, :] = (narrow[at, :] * slope_m[layer, at, :]).astype(BF16)

        chunks(2 * rows, slope)
        if layer == 0:
            tall_1.advance()
        spans = [ends(s, skip) for s in range(2)]

        def joined_rows(read, side):
            return jnp.concatenate([read(spans[s][side]) for s in range(2)], axis=0)

        def read_hidden(at, layer=layer):
            return hidden[layer, at, :]

        def read_grad(at):
            return grad_v[at, :]

        place(
            layer,
            0,
            0,
            grad_dot(joined_rows(read_hidden, 1), joined_rows(read_grad, 0)),
            per_chip,
        )
        place(layer, 0, per_chip, grad_dot(hidden[layer], grad_v[...]), per_chip)
        place(
            layer,
            0,
            2 * per_chip,
            grad_dot(joined_rows(read_hidden, 0), joined_rows(read_grad, 1)),
            per_chip,
        )
        if layer == 0:
            wide_1.advance()
        (wide_0, wide_1)[layer].advance()
        for s in range(2):
            narrow[strand(s), :] = dot_t(grad_v[strand(s), :], w_conv[layer, 1])
            after, before = ends(s, skip)
            narrow[before, :] += dot_t(grad_v[after, :], w_conv[layer, 0])
            narrow[after, :] += dot_t(grad_v[before, :], w_conv[layer, 2])

        def slope_back(at, layer=layer):
            grad_v[at, :] = (narrow[at, :] * slope_h[layer, at, :]).astype(BF16)

        chunks(2 * rows, slope_back)
        if layer == 0:
            wide_1.advance()
            tall_1.advance()
        (wide_0, wide_1)[layer].advance()
        place(layer, 1, 0, grad_dot(stream[layer], grad_v[...]), 2 * per_chip)
        if layer == 1:
            tall_1.advance()
            for s in range(2):
                wide[strand(s), :] = dot_t(grad_v[strand(s), :], w_in[layer])

            def renew(at):
                cot[at, :] = (cot[at, :].astype(F32) + wide[at, :]).astype(BF16)

            chunks(2 * rows, renew)
    tall_0.advance()
    for scatter in (wide_1, tall_1, wide_0, tall_0, tall_1, wide_0, tall_0, wide_0, tall_0, tall_0):
        scatter.advance()
    for scatter in (wide_1, tall_1, wide_0, tall_0):
        assert scatter.stage == 5
        scatter.finish()
    (wide_final, tall_final) = (chunk_refs[0][-1], chunk_refs[1][-1])
    limit = wide_final.shape[2]
    result[:, :, :limit, :] = wide_final[...]
    result[:, :, limit:, :] = tall_final[...]


def deliver(limit, per_chip, result, out_in, out_conv, out_out):
    core = lax.axis_index("seq") % 2
    hid = result.shape[3]
    own = per_chip // 2
    height = result.shape[2] - limit

    def rows_of(layer, base, size, start, count):
        pieces = []
        for half in range(2):
            low_row = max(start, half * size)
            high_row = min(start + count, (half + 1) * size)
            if low_row < high_row:
                offset = base - half * size
                pieces.append(result[layer, half, offset + low_row : offset + high_row, :])
        return pieces[0] if len(pieces) == 1 else jnp.concatenate(pieces, axis=0)

    for c in range(2):

        @pl.when(core == c)
        def _(c=c):
            for layer in range(2):
                out_in[layer] = rows_of(layer, limit, height, c * per_chip, per_chip)
                for t in range(3):
                    out_conv[t, :, layer, :] = rows_of(layer, 0, limit, t * per_chip + c * own, own)
                for t in range(2):
                    out_out[:, layer, t * hid : (t + 1) * hid] = rows_of(
                        layer, 0, limit, (3 + t) * per_chip + c * own, own
                    )


def local(features, targets, mappable, w_in, w_conv, w_out, w_head):
    rows, channels = features.shape
    n = lax.axis_size("seq")
    links = rows * n // FIRST_DILATION
    hid = w_in.shape[2]
    tracks = targets.shape[1]
    per_chip = 2 * hid // n
    heights = [(5 * per_chip + 31) // 32 * 16, (2 * per_chip + 31) // 32 * 16]
    mappable = jnp.broadcast_to(mappable[:, None], (rows, LANES))
    both = 2 * rows
    vmem = pl.BlockSpec(memory_space=pltpu.VMEM)
    hbm = pl.BlockSpec(memory_space=pl.ANY)
    chunk_shapes = []
    for height in heights:
        quad = (links, 2, 2, height, hid)
        chunk_shapes += [
            pltpu.VMEM((2, 2) + quad, F32),
            pltpu.VMEM((2,) + quad, BF16),
            pltpu.VMEM((2,) + quad, BF16),
            pltpu.VMEM((2, links, 2, height, hid), BF16),
            pltpu.VMEM((2, links, 2, height, hid), BF16),
            pltpu.VMEM((2, links, height, hid), BF16),
            pltpu.VMEM((2, links, height, hid), BF16),
            pltpu.VMEM((2, links, height, hid), BF16),
            pltpu.VMEM((2, links, height, hid), BF16),
            pltpu.VMEM((2, 2, height, hid), F32),
        ]
    result = pl.pallas_call(
        functools.partial(kernel, n),
        out_shape=jax.ShapeDtypeStruct((2, 2, sum(heights), hid), F32),
        in_specs=[vmem, vmem, vmem, hbm, hbm, hbm, hbm],
        out_specs=vmem,
        scratch_shapes=[
            pltpu.VMEM(w_in.shape, BF16),
            pltpu.VMEM(w_conv.shape, BF16),
            pltpu.VMEM(w_out.shape, BF16),
            pltpu.VMEM(w_head.shape, BF16),
            pltpu.VMEM((3, both, channels), BF16),
            pltpu.VMEM((rows, tracks + LANES), BF16),
            pltpu.VMEM((rows, tracks + LANES), BF16),
            pltpu.VMEM((2, both, hid), BF16),
            pltpu.VMEM((2, both, hid), F32),
            pltpu.VMEM((2, both, hid), BF16),
            pltpu.VMEM((2, both, hid), F32),
            pltpu.VMEM((both, channels), BF16),
            pltpu.VMEM((both, hid), BF16),
            pltpu.VMEM((both, hid), F32),
            pltpu.VMEM((both, channels), F32),
            pltpu.VMEM((rows, channels), BF16),
            pltpu.VMEM((rows, tracks), BF16),
            *chunk_shapes,
            pltpu.SemaphoreType.DMA((4,)),
            pltpu.SemaphoreType.DMA((2, links)),
            pltpu.SemaphoreType.DMA((2, links)),
            pltpu.SemaphoreType.DMA((4, 3 + links)),
            pltpu.SemaphoreType.DMA((4, 3 + links)),
        ],
        compiler_params=pltpu.CompilerParams(
            collective_id=0, has_side_effects=True, vmem_limit_bytes=60 * 1024 * 1024
        ),
    )(features, targets, mappable, w_in, w_conv, w_out, w_head)
    grad_in, grad_conv, grad_out = pl.pallas_call(
        functools.partial(deliver, heights[0], per_chip),
        out_shape=(
            jax.ShapeDtypeStruct((2, channels // n, hid), F32),
            jax.ShapeDtypeStruct((3, hid // n, 2, hid), F32),
            jax.ShapeDtypeStruct((hid // n, 2, channels), F32),
        ),
        in_specs=[vmem],
        out_specs=(vmem, vmem, vmem),
    )(result)
    return (grad_in, jnp.transpose(grad_conv, (2, 0, 1, 3)), jnp.transpose(grad_out, (1, 0, 2)))


def solution(mesh):
    in_specs = (
        P(("grp", "seq"), None),
        P(("grp", "seq"), None),
        P(("grp", "seq")),
        P(),
        P(),
        P(),
        P(),
    )
    out_specs = (P("grp", "seq", None), P("grp", None, "seq", None), P("grp", "seq", None))
    return jax.shard_map(local, mesh=mesh, in_specs=in_specs, out_specs=out_specs, check_vma=False)
```

time: 79 us -> 74.2 us (0.939)
  local copies, waits for them, and re-layouts: 4.81 us -> 1.43 us
  other arithmetic: 2.77 us -> 0 us
  Pallas kernels: 70.5 us -> 71.9 us
    pallas_call x2 -> x0, local copies, waits for them, and re-layouts: 3.19 us -> none  [local(): pl.pallas_call(functools.partial(kernel, n), out_shape=(jax.ShapeDtypeStr...]
    another operation x2 -> x0, other arithmetic: 1.92 us -> none
    unnamed x1 -> x0, local copies, waits for them, and re-layouts: 1.52 us -> none
    pallas_call x1 -> x2, Pallas kernels: 70.5 us -> 71.9 us  [the longest x1 70.1 us: local(): pl.pallas_call(functools.partial(kernel, n), out_shape=jax.ShapeDtypeStru...]
    broadcast_in_dim x1, local copies, waits for them, and re-layouts: 0.1 us -> 1.43 us  [local(): mappable = jnp.broadcast_to(mappable[:, None], (rows, LANES))]
    concatenate x1 -> x0, other arithmetic: 0.85 us -> none  [local(): packed = jnp.concatenate([targets, extra], axis=1).astype(BF16)]
where the time goes in v2:
time: 74.2 us; the launch traced here: 74 us
  Pallas kernels  71.9 us (97%)
  local copies, waits for them, and re-layouts  1.43 us (2%)
    pallas_call x1, Pallas kernels, local(): pl.pallas_call(functools.partial(kernel, n), out_shape=jax.ShapeDtypeStru...  70.1 us
    pallas_call x1, Pallas kernels, local(): pl.pallas_call(functools.partial(deliver, heights[0], per_chip), out_shap...  1.81 us

profile of v2, /device:TPU:0, one launch (start us, length us, event | category | flops | bytes accessed | tf_op | source)
XLA Modules:
  0.0 74.0 jit_solution(13416097324436251301)
XLA Ops:
  0.6 1.4 %broadcast_in_dim.2.refs_2_ = s32[256,128]{1,0:T(8,128)} broadcast(s32[256]{0:T(256)} %param.9), dimensions={0} | broadcast | bytes 132096 | tf_op jit(solution)/shard_map/broadcast_in_dim | solution.py:421
  2.1 70.1 %shard_map.94.result = f32[2,2,96,384]{3,2,1,0:T(8,128)} custom-call(bf16[256,768]{1,0:T(8,128)(2,1)} %refs_0_.1, s32[256,896]{1,0:T(8,128)} %refs_1_.1, s32[256,128]{1,0:T(8,128)} %broadcast_in_dim.2.refs_2_, bf16[2,768,384]{2,1,0:T(8,128)(2,1)} %refs_3_.1, bf16[2,3,384,384]{3,2,1,0:T(8,128)(2,1)} %refs_4_.1, bf16[2,384,768]{2,1,0:T(8,128)(2,1)} %refs_5_.1, ...), custom_call_target="tpu_custom_call" | custom-call | tf_op jit(solution)/shard_map/pallas_call | solution.py:440
  72.2 1.8 %shard_map.95 = (f32[2,24,384]{2,1,0:T(8,128)}, f32[3,12,2,384]{3,2,1,0:T(2,128)}, f32[12,2,768]{2,1,0:T(2,128)}) custom-call(f32[2,2,96,384]{3,2,1,0:T(8,128)} %shard_map.94.result), custom_call_target="tpu_custom_call" | custom-call | tf_op jit(solution)/shard_map/pallas_call | solution.py:474

commit v3 on v2

--- a/solution.py
+++ b/solution.py
@@ -369,7 +369,7 @@
 
             chunks(2 * rows, renew)
     tall_0.advance()
-    for scatter in (wide_1, tall_1, wide_0, tall_0, tall_1, wide_0, tall_0, wide_0, tall_0, tall_0):
+    for scatter in (tall_0, wide_1, tall_1, wide_0, tall_1, wide_0, tall_0, wide_0, tall_0, tall_0):
         scatter.advance()
     for scatter in (wide_1, tall_1, wide_0, tall_0):
         assert scatter.stage == 5

time: 74.2 us -> 73.2 us (0.987)
  Pallas kernels: 71.9 us -> 71 us
    pallas_call x1, Pallas kernels: 70.1 us -> 69.2 us  [local(): pl.pallas_call(functools.partial(kernel, n), out_shape=jax.ShapeDtypeStru...]
where the time goes in v3:
time: 73.2 us; the launch traced here: 73 us
  Pallas kernels  71 us (97%)
  local copies, waits for them, and re-layouts  1.43 us (2%)
    pallas_call x1, Pallas kernels, local(): pl.pallas_call(functools.partial(kernel, n), out_shape=jax.ShapeDtypeStru...  69.2 us
    pallas_call x1, Pallas kernels, local(): pl.pallas_call(functools.partial(deliver, heights[0], per_chip), out_shap...  1.81 us

profile of v3, /device:TPU:0, one launch (start us, length us, event | category | flops | bytes accessed | tf_op | source)
XLA Modules:
  0.0 73.0 jit_solution(7778528584481229820)
XLA Ops:
  0.6 1.4 %broadcast_in_dim.2.refs_2_ = s32[256,128]{1,0:T(8,128)} broadcast(s32[256]{0:T(256)} %param.9), dimensions={0} | broadcast | bytes 132096 | tf_op jit(solution)/shard_map/broadcast_in_dim | solution.py:421
  2.1 69.2 %shard_map.94.result = f32[2,2,96,384]{3,2,1,0:T(8,128)} custom-call(bf16[256,768]{1,0:T(8,128)(2,1)} %refs_0_.1, s32[256,896]{1,0:T(8,128)} %refs_1_.1, s32[256,128]{1,0:T(8,128)} %broadcast_in_dim.2.refs_2_, bf16[2,768,384]{2,1,0:T(8,128)(2,1)} %refs_3_.1, bf16[2,3,384,384]{3,2,1,0:T(8,128)(2,1)} %refs_4_.1, bf16[2,384,768]{2,1,0:T(8,128)(2,1)} %refs_5_.1, ...), custom_call_target="tpu_custom_call" | custom-call | tf_op jit(solution)/shard_map/pallas_call | solution.py:440
  71.2 1.8 %shard_map.95 = (f32[2,24,384]{2,1,0:T(8,128)}, f32[3,12,2,384]{3,2,1,0:T(2,128)}, f32[12,2,768]{2,1,0:T(2,128)}) custom-call(f32[2,2,96,384]{3,2,1,0:T(8,128)} %shard_map.94.result), custom_call_target="tpu_custom_call" | custom-call | tf_op jit(solution)/shard_map/pallas_call | solution.py:474
